TPU v7x, 32 devices: a whole 2x2x4 slice. The times are simulated.
32 devices in a mesh: dp: 4 (over y, core), fsdp: 8 (over z, x).
Axes of the slice: x: 2, y: 2, z: 4, core: 2. Of those that a mesh axis runs over, the one named last changes fastest.
Arguments:
- hidden_in: bfloat16 [2, 32, 1024, 576], P(None, ('dp', 'fsdp')), may hold values from -0.59765625 to 0.59765625
- seg_ids: int32 [2, 32, 1024], P(None, ('dp', 'fsdp')), may hold values from 0 to 7, never falling along the last dimension, each value on 1 to 512 neighbouring positions
- out_grad: bfloat16 [2, 32, 1024, 576], P(None, ('dp', 'fsdp')), may hold values from -6 to 6
- gains: float32 [2, 576], P(None, 'fsdp'), may hold values from 0.5 to 1.5
- matrices: float32 [576, 6144], P('fsdp'), may hold values from -8 to 8
- gain_momentum: float32 [2, 576], P(None, 'fsdp'), may hold values from -0.3 to 0.3
- mat_momentum: float32 [576, 6144], P('fsdp'), may hold values from -0.12 to 0.12
Outputs:
- out_hidden: bfloat16 [2, 32, 1024, 576], P(None, ('dp', 'fsdp'))
- in_grad: float32 [2, 32, 1024, 576], P(None, ('dp', 'fsdp'))
- matrix_grad: float32 [576, 6144], P('fsdp')
- gain_grad: float32 [2, 576], P(None, 'fsdp')
- new_mat_momentum: float32 [576, 6144], P('fsdp')
- new_gain_momentum: float32 [2, 576], P(None, 'fsdp')
- new_matrices: float32 [576, 6144], P('fsdp')
- new_gains: float32 [2, 576], P(None, 'fsdp')
Inputs may be any that keep to these rules, and one draw needn't show every extreme that they name: `seg_ids`: within a sequence segment numbers never fall; a document holds at most 512 tokens.
All inputs are finite; a program needn't handle non-finite values.
Results may differ from a plain program's by a relative error of at most 0.01.
The roundings to bfloat16 on the way count: a program that leaves them out, or rounds other values in their place, can miss the bound.
Values may be sent and summed in bfloat16 or wider, within the bound.
A program may use at most 384 MiB of HBM per device.

v0:
```python
import math
import jax
import jax.numpy as jnp
from jax import lax
from jax.sharding import PartitionSpec as P

D = 576
HEADS = 9
KVH = 3
HD = 64
FF = 1536
QB = 512
NS_STEPS = 5
HIGH = lax.Precision.HIGHEST
EPS_NORM = 1e-05
ROPE_BASE = 100000.0
MOMENT = 0.95
LEARN = 0.05
GAIN_LEARN = 0.1
COEF_A = 3.4445
COEF_B = -4.775
COEF_C = 2.0315
DIMS_ROWS = (((0,), (0,)), ((), ()))
DIMS_COLS = (((1,), (1,)), ((), ()))


def rope_tables(segment):
    seq_len = segment.shape[0]
    token_index = jnp.arange(seq_len, dtype=jnp.int32)
    first_mark = jnp.concatenate([jnp.ones((1,), dtype=bool), segment[1:] != segment[:-1]])
    start_index = lax.cummax(jnp.where(first_mark, token_index, 0), axis=0)
    offset = (token_index - start_index).astype(jnp.float32)
    inverse = 1.0 / ROPE_BASE ** (jnp.arange(0, HD, 2, dtype=jnp.float32) / HD)
    angle = offset[:, None] * inverse[None, :]
    return (jnp.cos(angle)[:, None, :], jnp.sin(angle)[:, None, :])


def rotate(values, cosine, sine):
    half_dim = values.shape[-1] // 2
    first_half = values[..., :half_dim]
    second_half = values[..., half_dim:]
    return jnp.concatenate(
        [first_half * cosine - second_half * sine, second_half * cosine + first_half * sine],
        axis=-1,
    )


def rotate_back(grads, cosine, sine):
    half_dim = grads.shape[-1] // 2
    first_half = grads[..., :half_dim]
    second_half = grads[..., half_dim:]
    return jnp.concatenate(
        [first_half * cosine + second_half * sine, second_half * cosine - first_half * sine],
        axis=-1,
    )


def attention_scores(query_blk, key_rows, segment, start_row, stop_row):
    scores = (
        jnp.einsum("qkgd,tkd->kgqt", query_blk, key_rows, preferred_element_type=jnp.float32)
        * 0.125
    )
    query_pos = start_row + jnp.arange(stop_row - start_row, dtype=jnp.int32)
    key_pos = jnp.arange(stop_row, dtype=jnp.int32)
    allowed = (key_pos[None, :] <= query_pos[:, None]) & (
        segment[:stop_row][None, :] == segment[start_row:stop_row][:, None]
    )
    return (scores, allowed)


def forward_pass(inputs, segment, weights, gain_pair):
    seq_len = inputs.shape[0]
    kv_cols = KVH * HD
    group_size = HEADS // KVH
    block_rows = min(QB, seq_len)
    cosine, sine = rope_tables(segment)
    r_one = lax.rsqrt(jnp.mean(inputs * inputs, axis=-1, keepdims=True) + EPS_NORM)
    u_one = inputs * r_one
    a_low = (u_one * gain_pair[0]).astype(jnp.bfloat16)
    projected = jnp.dot(a_low, weights[:, : D + 2 * kv_cols], preferred_element_type=jnp.float32)
    query_rot = (
        rotate(projected[:, :D].reshape(seq_len, HEADS, HD), cosine, sine)
        .astype(jnp.bfloat16)
        .reshape(seq_len, KVH, group_size, HD)
    )
    key_rot = rotate(projected[:, D : D + kv_cols].reshape(seq_len, KVH, HD), cosine, sine).astype(
        jnp.bfloat16
    )
    value_low = projected[:, D + kv_cols :].astype(jnp.bfloat16).reshape(seq_len, KVH, HD)
    head_out = []
    log_sums = []
    for block_id in range(seq_len // block_rows):
        start_row = block_id * block_rows
        stop_row = start_row + block_rows
        scores, allowed = attention_scores(
            query_rot[start_row:stop_row], key_rot[:stop_row], segment, start_row, stop_row
        )
        scores = jnp.where(allowed, scores, -1e30)
        row_max = jnp.max(scores, axis=-1, keepdims=True)
        exponent = jnp.exp(scores - row_max)
        row_total = jnp.sum(exponent, axis=-1, keepdims=True)
        probs_low = (exponent / row_total).astype(jnp.bfloat16)
        head_out.append(
            jnp.einsum(
                "kgqt,tkd->qkgd",
                probs_low,
                value_low[:stop_row],
                preferred_element_type=jnp.float32,
            ).reshape(block_rows, D)
        )
        log_sums.append(row_max + jnp.log(row_total))
    mixed_low = jnp.concatenate(head_out, axis=0).astype(jnp.bfloat16)
    middle = inputs + jnp.dot(
        mixed_low, weights[:, D + 2 * kv_cols : FF], preferred_element_type=jnp.float32
    )
    r_two = lax.rsqrt(jnp.mean(middle * middle, axis=-1, keepdims=True) + EPS_NORM)
    u_two = middle * r_two
    b_low = (u_two * gain_pair[1]).astype(jnp.bfloat16)
    gate_up = jnp.dot(b_low, weights[:, FF : 3 * FF], preferred_element_type=jnp.float32)
    gate_pre = gate_up[:, :FF]
    up_pre = gate_up[:, FF:]
    inner_low = (jax.nn.silu(gate_pre) * up_pre).astype(jnp.bfloat16)
    result = middle + lax.dot_general(
        inner_low, weights[:, 3 * FF :], DIMS_COLS, preferred_element_type=jnp.float32
    )
    saved = (
        segment,
        cosine,
        sine,
        r_one,
        u_one,
        a_low,
        query_rot,
        key_rot,
        value_low,
        log_sums,
        mixed_low,
        r_two,
        u_two,
        b_low,
        gate_pre,
        up_pre,
        inner_low,
    )
    return (saved, result.astype(jnp.bfloat16))


def backward_pass(saved, cotangent, weights, gain_pair):
    (
        segment,
        cosine,
        sine,
        r_one,
        u_one,
        a_low,
        query_rot,
        key_rot,
        value_low,
        log_sums,
        mixed_low,
        r_two,
        u_two,
        b_low,
        gate_pre,
        up_pre,
        inner_low,
    ) = saved
    seq_len = cotangent.shape[0]
    kv_cols = KVH * HD
    group_size = HEADS // KVH
    block_rows = min(QB, seq_len)
    d_branch = cotangent.astype(jnp.bfloat16)
    grad_down = lax.dot_general(d_branch, inner_low, DIMS_ROWS, preferred_element_type=jnp.float32)
    d_inner = jnp.dot(d_branch, weights[:, 3 * FF :], preferred_element_type=jnp.float32)
    sigma = jax.nn.sigmoid(gate_pre)
    silu_val = gate_pre * sigma
    d_gate = (d_inner * up_pre * sigma * (1.0 + gate_pre * (1.0 - sigma))).astype(jnp.bfloat16)
    d_up = (d_inner * silu_val).astype(jnp.bfloat16)
    d_gate_up = jnp.concatenate([d_gate, d_up], axis=1)
    grad_gate_up = lax.dot_general(b_low, d_gate_up, DIMS_ROWS, preferred_element_type=jnp.float32)
    d_norm_two = lax.dot_general(
        d_gate_up, weights[:, FF : 3 * FF], DIMS_COLS, preferred_element_type=jnp.float32
    )
    grad_gain_two = jnp.sum(d_norm_two * u_two, axis=0)
    d_unit_two = d_norm_two * gain_pair[1]
    d_middle = (
        r_two * (d_unit_two - u_two * jnp.mean(d_unit_two * u_two, axis=-1, keepdims=True))
        + cotangent
    )
    d_attn = d_middle.astype(jnp.bfloat16)
    grad_out = lax.dot_general(mixed_low, d_attn, DIMS_ROWS, preferred_element_type=jnp.float32)
    d_mixed = lax.dot_general(
        d_attn, weights[:, D + 2 * kv_cols : FF], DIMS_COLS, preferred_element_type=jnp.float32
    ).astype(jnp.bfloat16)
    query_grads = []
    d_key = jnp.zeros((seq_len, KVH, HD), jnp.float32)
    d_value = jnp.zeros((seq_len, KVH, HD), jnp.float32)
    for block_id in range(seq_len // block_rows):
        start_row = block_id * block_rows
        stop_row = start_row + block_rows
        query_blk = query_rot[start_row:stop_row]
        scores, allowed = attention_scores(
            query_blk, key_rot[:stop_row], segment, start_row, stop_row
        )
        probs = jnp.where(allowed, jnp.exp(scores - log_sums[block_id]), 0.0)
        probs_low = probs.astype(jnp.bfloat16)
        d_out_blk = d_mixed[start_row:stop_row].reshape(block_rows, KVH, group_size, HD)
        d_probs = jnp.einsum(
            "qkgd,tkd->kgqt", d_out_blk, value_low[:stop_row], preferred_element_type=jnp.float32
        )
        d_scores = (probs * (d_probs - jnp.sum(d_probs * probs, axis=-1, keepdims=True))).astype(
            jnp.bfloat16
        )
        query_grads.append(
            jnp.einsum(
                "kgqt,tkd->qkgd", d_scores, key_rot[:stop_row], preferred_element_type=jnp.float32
            )
            * 0.125
        )
        d_key = d_key.at[:stop_row].add(
            jnp.einsum("kgqt,qkgd->tkd", d_scores, query_blk, preferred_element_type=jnp.float32)
            * 0.125
        )
        d_value = d_value.at[:stop_row].add(
            jnp.einsum("kgqt,qkgd->tkd", probs_low, d_out_blk, preferred_element_type=jnp.float32)
        )
    d_query_rot = jnp.concatenate(query_grads, axis=0).reshape(seq_len, HEADS, HD)
    d_query = rotate_back(d_query_rot, cosine, sine).reshape(seq_len, D)
    d_key_pre = rotate_back(d_key, cosine, sine).reshape(seq_len, kv_cols)
    d_project = jnp.concatenate(
        [d_query, d_key_pre, d_value.reshape(seq_len, kv_cols)], axis=1
    ).astype(jnp.bfloat16)
    grad_project = lax.dot_general(a_low, d_project, DIMS_ROWS, preferred_element_type=jnp.float32)
    d_norm_one = lax.dot_general(
        d_project, weights[:, : D + 2 * kv_cols], DIMS_COLS, preferred_element_type=jnp.float32
    )
    grad_gain_one = jnp.sum(d_norm_one * u_one, axis=0)
    d_unit_one = d_norm_one * gain_pair[0]
    d_input = (
        r_one * (d_unit_one - u_one * jnp.mean(d_unit_one * u_one, axis=-1, keepdims=True))
        + d_middle
    )
    grad_weights = jnp.concatenate([grad_project, grad_out, grad_gate_up, grad_down], axis=1)
    grad_gains = jnp.stack([grad_gain_one, grad_gain_two], axis=0)
    return (d_input, grad_weights, grad_gains)


def orthogonal(matrix):
    tall = matrix.shape[0] > matrix.shape[1]
    work = matrix.T if tall else matrix
    work = work / (jnp.sqrt(jnp.sum(work * work)) + 1e-07)
    for sweep_id in range(NS_STEPS):
        gram = jnp.dot(work, work.T, precision=HIGH)
        poly = COEF_B * gram + COEF_C * jnp.dot(gram, gram, precision=HIGH)
        work = COEF_A * work + jnp.dot(poly, work, precision=HIGH)
    if tall:
        work = work.T
    return work * (0.2 * math.sqrt(max(matrix.shape)))


def attention_block(block):
    kv_cols = KVH * HD
    bounds = [0, D, D + kv_cols, D + 2 * kv_cols, FF]
    pieces = [
        orthogonal(block[:, bounds[block_id] : bounds[block_id + 1]]) for block_id in range(4)
    ]
    return jnp.concatenate(pieces, axis=1)


def feed_block(block):
    return orthogonal(block)


def on_device(hidden_in, seg_ids, out_grad, gains, matrices, gain_momentum, mat_momentum):
    shard_rows = matrices.shape[0]
    total_cols = matrices.shape[1]
    full_rows = shard_rows * lax.axis_size("fsdp")
    total_tokens = (
        hidden_in.shape[0]
        * hidden_in.shape[1]
        * hidden_in.shape[2]
        * lax.axis_size("dp")
        * lax.axis_size("fsdp")
    )
    grad_scale = float(total_tokens) ** (-0.5)
    shard_low = matrices.astype(jnp.bfloat16)
    gain_low = gains.T.astype(jnp.bfloat16)

    def micro_step(running, element):
        inputs, segment, cotangent = element
        weights, gain_rows = (
            lax.all_gather(shard_low, "fsdp", axis=0, tiled=True),
            lax.all_gather(gain_low, "fsdp", axis=0, tiled=True),
        )
        gain_pair = gain_rows.astype(jnp.float32).T
        saved, result = forward_pass(inputs.astype(jnp.float32), segment, weights, gain_pair)
        weights_back, gain_back = (
            lax.all_gather(shard_low, "fsdp", axis=0, tiled=True),
            lax.all_gather(gain_low, "fsdp", axis=0, tiled=True),
        )
        gain_pair_back = gain_back.astype(jnp.float32).T
        d_input, grad_weights, grad_gains = backward_pass(
            saved, cotangent.astype(jnp.float32), weights_back, gain_pair_back
        )
        running = (running[0] + grad_weights, running[1] + grad_gains.T)
        return (running, (result, d_input))

    start_acc = (
        jnp.zeros((full_rows, total_cols), jnp.float32),
        jnp.zeros((full_rows, 2), jnp.float32),
    )
    totals, outputs = lax.scan(
        micro_step, start_acc, (hidden_in[:, 0], seg_ids[:, 0], out_grad[:, 0])
    )
    shard_weights, shard_gains = (
        lax.psum_scatter(totals[0], "fsdp", scatter_dimension=0, tiled=True),
        lax.psum_scatter(totals[1], "fsdp", scatter_dimension=0, tiled=True),
    )
    summed_weights, summed_gains = lax.psum((shard_weights, shard_gains), "dp")
    matrix_grad = summed_weights * grad_scale
    gain_grad = (summed_gains * grad_scale).T
    new_mat_momentum = MOMENT * mat_momentum + matrix_grad
    new_gain_momentum = MOMENT * gain_momentum + gain_grad
    look = matrix_grad + MOMENT * new_mat_momentum
    owner_group = lax.axis_index("dp")
    block_cols = total_cols // 4
    own_block = lax.dynamic_slice_in_dim(look, owner_group * block_cols, block_cols, 1)
    whole_block, whole_gain_mom = (
        lax.all_gather(own_block, "fsdp", axis=0, tiled=True),
        lax.all_gather(new_gain_momentum.T, "fsdp", axis=0, tiled=True),
    )
    orthogonal_block = lax.switch(
        owner_group, [attention_block, feed_block, feed_block, feed_block], whole_block
    )
    own_rows = lax.dynamic_slice_in_dim(
        orthogonal_block, lax.axis_index("fsdp") * shard_rows, shard_rows, 0
    )
    update_rows = lax.all_gather(own_rows, "dp", axis=1, tiled=True)
    new_matrices = matrices - LEARN * update_rows
    spread = lax.rsqrt(jnp.mean(whole_gain_mom * whole_gain_mom, axis=0, keepdims=True) + 1e-06)
    new_gains = gains - GAIN_LEARN * new_gain_momentum * spread.T
    out_hidden = outputs[0][:, None]
    in_grad = outputs[1][:, None]
    return (
        out_hidden,
        in_grad,
        matrix_grad,
        gain_grad,
        new_mat_momentum,
        new_gain_momentum,
        new_matrices,
        new_gains,
    )


def solution(mesh):
    in_specs = (
        P(None, ("dp", "fsdp"), None, None),
        P(None, ("dp", "fsdp"), None),
        P(None, ("dp", "fsdp"), None, None),
        P(None, "fsdp"),
        P("fsdp", None),
        P(None, "fsdp"),
        P("fsdp", None),
    )
    out_specs = (
        P(None, ("dp", "fsdp"), None, None),
        P(None, ("dp", "fsdp"), None, None),
        P("fsdp", None),
        P(None, "fsdp"),
        P("fsdp", None),
        P(None, "fsdp"),
        P("fsdp", None),
        P(None, "fsdp"),
    )
    return jax.shard_map(
        on_device, mesh=mesh, in_specs=in_specs, out_specs=out_specs, check_vma=False
    )
```

profile of v0, /device:TPU:0, one launch (start us, length us, event | category | flops | bytes accessed | tf_op | source)
XLA Modules:
  0.0 1261.2 jit_solution(15243894904164791844)
XLA Ops:
  11.0 648.6 %while.26 = (s32[]{:T(128)}, f32[576,6144]{1,0:T(8,128)}, f32[576,2]{0,1:T(2,128)}, bf16[2,1024,576]{1,2,0:T(8,128)(2,1)}, f32[2,1024,576]{1,2,0:T(8,128)}, /*in...) while((s32[]{:T(128)}, f32[576,6144]{1,0:T(8,128)}, ...), condition=%wide.region_15.16_spmd.clone, body=%wide.region_0.15_spmd.clone.sunk | while | flops 27494117376 | bytes 824622656 | solution.py:312
  12.8 22.6 %all-gather.4 = bf16[8,72,2]{1,2,0:T(2,128)(2,1)S(1)} all-gather(bf16[1,72,2]{1,2,0:T(2,128)(2,1)S(1)} %bitcast.639), channel_id=1, replica_groups=mesh['dp'=4,'fsdp'=8] {'fsdp'}, dimensions={0}, use_global_device_ids=true | all-gather | bytes 2592 | tf_op jit(solution)/shard_map/while/body/eval_jaxpr/all_gather | solution.py:293
  38.7 87.1 %all-gather.13.cloned.1.call-done = bf16[576,6144]{1,0:T(8,128)(2,1)} async-done(((bf16[72,6144]{1,0:T(8,128)(2,1)}), bf16[576,6144]{1,0:T(8,128)(2,1)}) %all-gather.13.cloned.1.call-update) | async-done | bytes 7077904 | tf_op jit(solution)/shard_map/while/body/eval_jaxpr/all_gather | solution.py:292
  148.2 10.2 fusion.692
  171.3 12.0 fusion.698
  223.5 11.2 fusion.705
  245.4 13.3 %fusion.702 = (f32[3,3,512]{2,1,0:T(4,128)S(1)}, f32[3,1024,512,3]{2,1,3,0:T(8,128)}) fusion(f32[3,1024,512,3]{2,1,3,0:T(8,128)} %get-tuple-element.469, f32[3,3,512]{2,1,0:T(4,128)S(1)} %copy-done.33, pred[512,1024]{0,1:T(8,128)(4,1)S(1)} %fusion.688, bf16[1024,3,64,1]{0,2,3,1:T(8,128)(2,1)S(1)} %bitcast.620, bf16[512,3,3,64]{0,3,2,1:T(8,128)(2,1)S(1)} %bitcast.617), kind=kOutput, calls=%fused_computation.301.clone.1 | convolution fusion | flops 627568128 | bytes 39292928 | tf_op jit(solution)/shard_map/while/body/eval_jaxpr/qkgd,tkd->kgqt/dot_general | solution.py:208
  267.1 13.5 %fusion.703 = bf16[3,3,512,1024]{2,3,1,0:T(8,128)(2,1)S(1)} fusion(f32[3,1024,512,3]{2,1,3,0:T(8,128)} %get-tuple-element.484, f32[3,1024,512,3]{2,1,3,0:T(8,128)} %get-tuple-element.469, f32[3,3,512]{2,1,0:T(4,128)S(1)} %get-tuple-element.485, f32[3,3,512]{2,1,0:T(4,128)S(1)} %copy-done.33, pred[512,1024]{0,1:T(8,128)(4,1)S(1)} %fusion.688), kind=kLoop, calls=%fused_computation.303.clone.1 | loop fusion | flops 28311552 | bytes 47747072 | tf_op jit(solution)/shard_map/while/body/eval_jaxpr/convert_element_type | solution.py:211
  294.7 15.7 %concatenate.101 = f32[576,6144]{1,0:T(8,128)} concatenate(f32[576,960]{1,0:T(8,128)} %fusion.710, f32[576,576]{1,0:T(8,128)} %fusion.711, f32[576,3072]{1,0:T(8,128)} %fusion.712, f32[576,1536]{1,0:T(8,128)} %fusion.713), dimensions={1} | concatenate | bytes 28311552 | tf_op jit(solution)/shard_map/while/body/eval_jaxpr/concatenate | solution.py:243
  310.5 11.6 select_add_fusion.2
  333.2 18.2 %all-gather.4 = bf16[8,72,2]{1,2,0:T(2,128)(2,1)S(1)} all-gather(bf16[1,72,2]{1,2,0:T(2,128)(2,1)S(1)} %bitcast.639), channel_id=1, replica_groups=mesh['dp'=4,'fsdp'=8] {'fsdp'}, dimensions={0}, use_global_device_ids=true | all-gather | bytes 2592 | tf_op jit(solution)/shard_map/while/body/eval_jaxpr/all_gather | solution.py:293
  354.7 86.7 %all-gather.13.cloned.1.call-done = bf16[576,6144]{1,0:T(8,128)(2,1)} async-done(((bf16[72,6144]{1,0:T(8,128)(2,1)}), bf16[576,6144]{1,0:T(8,128)(2,1)}) %all-gather.13.cloned.1.call-update) | async-done | bytes 7077904 | tf_op jit(solution)/shard_map/while/body/eval_jaxpr/all_gather | solution.py:292
  486.7 11.4 fusion.698
  538.6 11.2 fusion.705
  560.5 13.3 %fusion.702 = (f32[3,3,512]{2,1,0:T(4,128)S(1)}, f32[3,1024,512,3]{2,1,3,0:T(8,128)}) fusion(f32[3,1024,512,3]{2,1,3,0:T(8,128)} %get-tuple-element.469, f32[3,3,512]{2,1,0:T(4,128)S(1)} %copy-done.33, pred[512,1024]{0,1:T(8,128)(4,1)S(1)} %fusion.688, bf16[1024,3,64,1]{0,2,3,1:T(8,128)(2,1)S(1)} %bitcast.620, bf16[512,3,3,64]{0,3,2,1:T(8,128)(2,1)S(1)} %bitcast.617), kind=kOutput, calls=%fused_computation.301.clone.1 | convolution fusion | flops 627568128 | bytes 39292928 | tf_op jit(solution)/shard_map/while/body/eval_jaxpr/qkgd,tkd->kgqt/dot_general | solution.py:208
  582.2 13.5 %fusion.703 = bf16[3,3,512,1024]{2,3,1,0:T(8,128)(2,1)S(1)} fusion(f32[3,1024,512,3]{2,1,3,0:T(8,128)} %get-tuple-element.484, f32[3,1024,512,3]{2,1,3,0:T(8,128)} %get-tuple-element.469, f32[3,3,512]{2,1,0:T(4,128)S(1)} %get-tuple-element.485, f32[3,3,512]{2,1,0:T(4,128)S(1)} %copy-done.33, pred[512,1024]{0,1:T(8,128)(4,1)S(1)} %fusion.688), kind=kLoop, calls=%fused_computation.303.clone.1 | loop fusion | flops 28311552 | bytes 47747072 | tf_op jit(solution)/shard_map/while/body/eval_jaxpr/convert_element_type | solution.py:211
  609.8 15.7 %concatenate.101 = f32[576,6144]{1,0:T(8,128)} concatenate(f32[576,960]{1,0:T(8,128)} %fusion.710, f32[576,576]{1,0:T(8,128)} %fusion.711, f32[576,3072]{1,0:T(8,128)} %fusion.712, f32[576,1536]{1,0:T(8,128)} %fusion.713), dimensions={1} | concatenate | bytes 28311552 | tf_op jit(solution)/shard_map/while/body/eval_jaxpr/concatenate | solution.py:243
  625.6 15.6 %select_add_fusion.2 = f32[576,6144]{1,0:T(8,128)} fusion(f32[576,6144]{1,0:T(8,128)} %concatenate.101, f32[576,6144]{1,0:T(8,128)} %get-tuple-element.514, pred[]{:T(512)S(6)} %compare.47), kind=kLoop, calls=%fused_computation.312.clone.1 | loop fusion | flops 7077888 | bytes 42467328 | tf_op jit(solution)/shard_map/while/body/eval_jaxpr/add | solution.py:305
  660.3 231.0 %reduce-scatter.3.cloned.1.call-done = f32[72,6144]{1,0:T(8,128)} async-done(((f32[576,6144]{1,0:T(8,128)}), f32[72,6144]{1,0:T(8,128)}) %reduce-scatter.3.cloned.1.call-update) | async-done | bytes 1769488 | tf_op jit(solution)/shard_map/reduce_scatter | solution.py:316
  891.4 47.2 %all-reduce.5.cloned.1.call-done = f32[72,6144]{1,0:T(8,128)} async-done(((f32[72,6144]{1,0:T(8,128)}), f32[72,6144]{1,0:T(8,128)}) %all-reduce.5.cloned.1.call-update) | async-done | bytes 1769488 | tf_op jit(solution)/shard_map/psum | solution.py:319
  943.1 64.5 %all-gather.9.cloned.1.call-done = f32[576,1536]{1,0:T(8,128)} async-done(((f32[72,1536]{1,0:T(8,128)}), f32[576,1536]{1,0:T(8,128)}) %all-gather.9.cloned.1.call-update) | async-done | bytes 3538960 | tf_op jit(solution)/shard_map/all_gather | solution.py:329
  1007.6 196.8 %conditional.1 = (f32[576,1536]{1,0:T(8,128)S(1)}) conditional(s32[]{:T(128)} %clamp.3, f32[576,1536]{1,0:T(8,128)} %all-gather.9.cloned.1.call-done, f32[576,1536]{1,0:T(8,128)} %all-gather.9.cloned.1.call-done, f32[576,1536]{1,0:T(8,128)} %all-gather.9.cloned.1.call-done, ...), branch_computations={%region_20.25_spmd, %region_25.27_spmd, %region_27.29_spmd, %regio... | conditional | flops 74772799488 | bytes 174001792 | solution.py:332
  1207.2 19.4 %all-reduce.2 = f32[576,2]{0,1:T(2,128)S(1)} all-reduce(f32[576,2]{0,1:T(2,128)S(1)} %copy-done.47), channel_id=3, replica_groups=mesh['dp'=4,'fsdp'=8] {'fsdp'}, use_global_device_ids=true, to_apply=%region_18.19.clone | all-reduce | flops 1152 | bytes 9216
  1233.0 16.3 %all-gather.1 = f32[8,72,2]{1,2,0:T(2,128)S(1)} all-gather(f32[1,72,2]{1,2,0:T(2,128)S(1)} %bitcast.640), channel_id=1, replica_groups=mesh['dp'=4,'fsdp'=8] {'fsdp'}, dimensions={0}, use_global_device_ids=true | all-gather | bytes 5184 | tf_op jit(solution)/shard_map/all_gather | solution.py:330
  (457 shorter events, 441.3 us)
Async XLA Ops:
  11.3 26.1 %copy-start.43 = (s32[2,1024]{1,0:T(2,128)}, s32[2,1024]{1,0:T(2,128)S(1)}, u32[]{:S(2)}) copy-start(s32[2,1024]{1,0:T(2,128)S(1)} %get-tuple-element.537) | copy-start | bytes 24580 | tf_op jit(solution)/shard_map/while
  11.3 114.5 %all-gather.13.cloned.1.call-start = ((), (), s32[]{:S(2)}) async-start(), calls=%async_computation.5 | async-start | bytes 7962624 | tf_op jit(solution)/shard_map/while/body/eval_jaxpr/all_gather | solution.py:292
  37.3 92.0 %copy-start.41 = (f32[576]{0:T(1024)}, f32[576]{0:T(1024)S(1)}, u32[]{:S(2)}) copy-start(f32[576]{0:T(1024)S(1)} %get-tuple-element.458) | copy-start | bytes 6916 | tf_op jit(solution)/shard_map/while
  37.3 92.0 %copy-start.34 = (f32[1024]{0:T(1024)}, f32[1024]{0:T(1024)S(1)}, u32[]{:S(2)}) copy-start(f32[1024]{0:T(1024)S(1)} %add_rsqrt_fusion.4) | copy-start | bytes 12292 | tf_op jit(solution)/shard_map/while
  38.2 92.6 %copy-start.6 = (f32[1024,32]{0,1:T(8,128)}, f32[1024,32]{0,1:T(8,128)S(1)}, u32[]{:S(2)}) copy-start(f32[1024,32]{0,1:T(8,128)S(1)} %get-tuple-element.463) | copy-start | bytes 393220 | tf_op jit(solution)/shard_map/while
  38.2 92.6 %copy-start.8 = (f32[1024,32]{0,1:T(8,128)}, f32[1024,32]{0,1:T(8,128)S(1)}, u32[]{:S(2)}) copy-start(f32[1024,32]{0,1:T(8,128)S(1)} %get-tuple-element.462) | copy-start | bytes 393220 | tf_op jit(solution)/shard_map/while
  171.2 38.8 %copy-start.18 = (f32[1024,576]{0,1:T(8,128)}, f32[1024,576]{0,1:T(8,128)S(1)}, u32[]{:S(2)}) copy-start(f32[1024,576]{0,1:T(8,128)S(1)} %get-tuple-element.475) | copy-start | bytes 7077892 | tf_op jit(solution)/shard_map/while
  331.7 21.8 %copy-start.43 = (s32[2,1024]{1,0:T(2,128)}, s32[2,1024]{1,0:T(2,128)S(1)}, u32[]{:S(2)}) copy-start(s32[2,1024]{1,0:T(2,128)S(1)} %get-tuple-element.537) | copy-start | bytes 24580 | tf_op jit(solution)/shard_map/while
  331.7 109.7 %all-gather.13.cloned.1.call-start = ((), (), s32[]{:S(2)}) async-start(), calls=%async_computation.5 | async-start | bytes 7962624 | tf_op jit(solution)/shard_map/while/body/eval_jaxpr/all_gather | solution.py:292
  353.4 91.5 %copy-start.41 = (f32[576]{0:T(1024)}, f32[576]{0:T(1024)S(1)}, u32[]{:S(2)}) copy-start(f32[576]{0:T(1024)S(1)} %get-tuple-element.458) | copy-start | bytes 6916 | tf_op jit(solution)/shard_map/while
  353.4 91.5 %copy-start.34 = (f32[1024]{0:T(1024)}, f32[1024]{0:T(1024)S(1)}, u32[]{:S(2)}) copy-start(f32[1024]{0:T(1024)S(1)} %add_rsqrt_fusion.4) | copy-start | bytes 12292 | tf_op jit(solution)/shard_map/while
  354.2 92.1 %copy-start.6 = (f32[1024,32]{0,1:T(8,128)}, f32[1024,32]{0,1:T(8,128)S(1)}, u32[]{:S(2)}) copy-start(f32[1024,32]{0,1:T(8,128)S(1)} %get-tuple-element.463) | copy-start | bytes 393220 | tf_op jit(solution)/shard_map/while
  354.2 92.1 %copy-start.8 = (f32[1024,32]{0,1:T(8,128)}, f32[1024,32]{0,1:T(8,128)S(1)}, u32[]{:S(2)}) copy-start(f32[1024,32]{0,1:T(8,128)S(1)} %get-tuple-element.462) | copy-start | bytes 393220 | tf_op jit(solution)/shard_map/while
  486.7 38.5 %copy-start.18 = (f32[1024,576]{0,1:T(8,128)}, f32[1024,576]{0,1:T(8,128)S(1)}, u32[]{:S(2)}) copy-start(f32[1024,576]{0,1:T(8,128)S(1)} %get-tuple-element.475) | copy-start | bytes 7077892 | tf_op jit(solution)/shard_map/while
  625.6 15.6 %copy-start.20 = (f32[1024,576]{0,1:T(8,128)S(1)}, f32[1024,576]{0,1:T(8,128)}, u32[]{:S(2)}) copy-start(f32[1024,576]{0,1:T(8,128)} %get-tuple-element.495) | copy-start | bytes 7077892 | tf_op jit(solution)/shard_map/while
  659.6 231.7 %reduce-scatter.3.cloned.1.call-start = ((), (), s32[]{:S(2)}) async-start(), calls=%async_computation.1 | async-start | bytes 15925248 | tf_op jit(solution)/shard_map/reduce_scatter | solution.py:316
  660.2 278.4 %copy-start.40 = (f32[72,6144]{1,0:T(8,128)S(1)}, f32[72,6144]{1,0:T(8,128)}, u32[]{:S(2)}) copy-start(f32[72,6144]{1,0:T(8,128)} %param.31) | copy-start | bytes 5308420
  660.2 278.4 %all-reduce.5.cloned.1.call-start = ((), (), s32[]{:S(2)}) async-start(), calls=%async_computation.2 | async-start | bytes 3538944 | tf_op jit(solution)/shard_map/psum | solution.py:319
  891.3 116.3 %all-gather.9.cloned.1.call-start = ((), (), s32[]{:S(2)}) async-start(), calls=%async_computation.3 | async-start | bytes 3981312 | tf_op jit(solution)/shard_map/all_gather | solution.py:329
  943.0 307.0 %all-gather.11.cloned.1.call-start = ((), (), s32[]{:S(2)}) async-start(), calls=%async_computation.4 | async-start | bytes 2211840 | tf_op jit(solution)/shard_map/all_gather | solution.py:338
  1007.6 199.6 %copy-start.47 = (f32[576,2]{0,1:T(2,128)S(1)}, f32[576,2]{0,1:T(2,128)}, u32[]{:S(2)}) copy-start(f32[576,2]{0,1:T(2,128)} %get-tuple-element.254) | copy-start | bytes 13828
  1007.6 224.8 %copy-start.52 = (f32[2,72]{1,0:T(2,128)S(1)}, f32[2,72]{1,0:T(2,128)}, u32[]{:S(2)}) copy-start(f32[2,72]{1,0:T(2,128)} %param.30) | copy-start | bytes 1732
  1007.6 241.8 %copy-start.51 = (f32[2,72]{1,0:T(2,128)S(1)}, f32[2,72]{1,0:T(2,128)}, u32[]{:S(2)}) copy-start(f32[2,72]{1,0:T(2,128)} %param.28) | copy-start | bytes 1732
  1233.0 20.5 %copy-start.50 = (f32[2,72]{1,0:T(2,128)}, f32[2,72]{1,0:T(2,128)S(1)}, u32[]{:S(2)}) copy-start(f32[2,72]{1,0:T(2,128)S(1)} %get-tuple-element.318) | copy-start | bytes 1732
  (96 other events, 541.4 us)
Sparse Core Ops, SparseCore 0:
  14.9 110.8 all-gather.12
  335.3 106.0 all-gather.12
Sparse Core Ops, SparseCore 1:
  663.8 227.5 reduce-scatter.2
  893.6 45.0 all-reduce.4
  943.1 64.4 all-gather.8
  1205.4 18.4 all-gather.10
where the time goes:
time: 1260 us
  waiting for transfers between devices  517 us (41%)
  matrix products  405 us (32%)
  other arithmetic  134 us (11%)
  blocking collectives  82.2 us (7%)
  local copies, waits for them, and re-layouts  63.8 us (5%)
  loops' own time  42.1 us (3%)
  between operations  16.6 us (1%)
    reduce_scatter x1, waiting for transfers between devices, on_device(): lax.psum_scatter(totals[0], 'fsdp', scatter_dimension=0, tiled=True)  231 us
    all_gather x2, waiting for transfers between devices, micro_step(): lax.all_gather(shard_low, 'fsdp', axis=0, tiled=True)  174 us
    all_gather x1, waiting for transfers between devices, on_device(): lax.all_gather(own_block, 'fsdp', axis=0, tiled=True)  64.5 us
    dot_general x20, matrix products, orthogonal(): gram = jnp.dot(work, work.T, precision=HIGH)  56.5 us
    dot_general x20, matrix products, orthogonal(): work = COEF_A * work + jnp.dot(poly, work, precision=HIGH)  54.7 us
    convert_element_type x4, other arithmetic, backward_pass(): (probs * (d_probs - jnp.sum(d_probs * probs, axis=-1, keepdims=True))).as...  49.4 us
    psum x1, waiting for transfers between devices, on_device(): summed_weights, summed_gains = lax.psum((shard_weights, shard_gains), 'dp')  47.2 us
    dot_general x20, matrix products, orthogonal(): poly = COEF_B * gram + COEF_C * jnp.dot(gram, gram, precision=HIGH)  46.2 us
  transfers between devices with their start and end apart: 6, of which 5 were waited for; matrix products, arithmetic and copies ran while one was open for 1% of the time, Pallas kernels for 0%

commit v1 on v0

--- a/solution.py
+++ b/solution.py
@@ -22,6 +22,12 @@
 COEF_C = 2.0315
 DIMS_ROWS = (((0,), (0,)), ((), ()))
 DIMS_COLS = (((1,), (1,)), ((), ()))
+
+
+def render_slices(x_in, chip_axis, array_axis):
+    return jnp.concatenate(
+        lax.all_to_all(jnp.stack(lax.axis_size(chip_axis) * [x_in], 0), chip_axis, 0, 0), array_axis
+    )
 
 
 def rope_tables(segment):
@@ -289,7 +295,7 @@
     def micro_step(running, element):
         inputs, segment, cotangent = element
         weights, gain_rows = (
-            lax.all_gather(shard_low, "fsdp", axis=0, tiled=True),
+            render_slices(shard_low, "fsdp", 0),
             lax.all_gather(gain_low, "fsdp", axis=0, tiled=True),
         )
         gain_pair = gain_rows.astype(jnp.float32).T

time: 1260 us -> 1570 us (1.25)
  blocking collectives: 82.2 us -> 396 us
  waiting for transfers between devices: 517 us -> 469 us
  starting transfers between devices: 0.26 us -> 24.3 us
  local copies, waits for them, and re-layouts: 63.8 us -> 80.6 us
    all_gather x2, blocking collectives: 40.8 us -> 354 us  [micro_step(): lax.all_gather(gain_low, 'fsdp', axis=0, tiled=True)]
    all_gather x2, waiting for transfers between devices: 174 us -> 0.01 us  [micro_step(): lax.all_gather(shard_low, 'fsdp', axis=0, tiled=True)]
    all_to_all x0 -> x2, waiting for transfers between devices: none -> 110 us  [render_slices(): lax.all_to_all(jnp.stack(lax.axis_size(chip_axis) * [x_in], 0), chip_axis...]
    all_to_all x0 -> x2, starting transfers between devices: none -> 24.1 us  [render_slices(): lax.all_to_all(jnp.stack(lax.axis_size(chip_axis) * [x_in], 0), chip_axis...]
  transfers between devices with their start and end apart: 6 -> 8, of which waited for: 5 -> 5; matrix products, arithmetic and copies ran while one was open for 1% -> 8% of each run, Pallas kernels for 0% -> 0%
where the time goes in v1:
time: 1570 us
  waiting for transfers between devices  469 us (30%)
  matrix products  399 us (25%)
  blocking collectives  396 us (25%)
  other arithmetic  141 us (9%)
  local copies, waits for them, and re-layouts  80.6 us (5%)
  loops' own time  42.2 us (3%)
  starting transfers between devices  24.3 us (2%)
  between operations  16.7 us (1%)
    all_gather x2, blocking collectives, micro_step(): lax.all_gather(gain_low, 'fsdp', axis=0, tiled=True)  354 us
    reduce_scatter x1, waiting for transfers between devices, on_device(): lax.psum_scatter(totals[0], 'fsdp', scatter_dimension=0, tiled=True)  245 us
    all_to_all x2, waiting for transfers between devices, render_slices(): lax.all_to_all(jnp.stack(lax.axis_size(chip_axis) * [x_in], 0), chip_axis...  110 us
    all_gather x1, waiting for transfers between devices, on_device(): lax.all_gather(own_block, 'fsdp', axis=0, tiled=True)  64.5 us
    dot_general x20, matrix products, orthogonal(): gram = jnp.dot(work, work.T, precision=HIGH)  56.9 us
    dot_general x20, matrix products, orthogonal(): work = COEF_A * work + jnp.dot(poly, work, precision=HIGH)  54.7 us
    convert_element_type x4, other arithmetic, backward_pass(): (probs * (d_probs - jnp.sum(d_probs * probs, axis=-1, keepdims=True))).as...  49.6 us
    psum x1, waiting for transfers between devices, on_device(): summed_weights, summed_gains = lax.psum((shard_weights, shard_gains), 'dp')  47.2 us
  transfers between devices with their start and end apart: 8, of which 5 were waited for; matrix products, arithmetic and copies ran while one was open for 8% of the time, Pallas kernels for 0%

profile of v1, /device:TPU:0, one launch (start us, length us, event | category | flops | bytes accessed | tf_op | source)
XLA Modules:
  0.0 1569.0 jit_solution(17242305922069696648)
XLA Ops:
  13.0 940.8 %while.26 = (s32[]{:T(128)}, f32[576,6144]{1,0:T(8,128)}, f32[576,2]{0,1:T(2,128)}, bf16[2,1024,576]{1,2,0:T(8,128)(2,1)}, f32[2,1024,576]{1,2,0:T(8,128)}, /*in...) while((s32[]{:T(128)}, f32[576,6144]{1,0:T(8,128)}, ...), condition=%wide.region_15.16_spmd.clone, body=%wide.region_0.15_spmd.clone.sunk | while | flops 27494117376 | bytes 895872512 | solution.py:318
  27.4 177.9 %all-gather.4 = bf16[8,72,2]{1,2,0:T(2,128)(2,1)S(1)} all-gather(bf16[1,72,2]{1,2,0:T(2,128)(2,1)} %bitcast.589), channel_id=1, replica_groups=mesh['dp'=4,'fsdp'=8] {'fsdp'}, dimensions={0}, use_global_device_ids=true | all-gather | bytes 2592 | tf_op jit(solution)/shard_map/while/body/eval_jaxpr/all_gather | solution.py:299
  210.4 55.9 %all-to-all-done = bf16[8,72,6144]{2,1,0:T(8,128)(2,1)} async-done(((bf16[8,72,6144]{2,1,0:T(8,128)(2,1)}), bf16[8,72,6144]{2,1,0:T(8,128)(2,1)}, u32[]{:S(2)}, u32[]{:S(2)}) %all-to-all-start) | async-done | bytes 7077920 | tf_op jit(solution)/shard_map/while/body/eval_jaxpr/all_to_all | solution.py:29
  326.0 10.7 multiply_convert_fusion.11
  366.6 11.2 fusion.705
  393.5 13.2 fusion.702
  415.1 13.6 fusion.703
  443.5 15.8 %concatenate.101 = f32[576,6144]{1,0:T(8,128)} concatenate(f32[576,960]{1,0:T(8,128)} %fusion.710, f32[576,576]{1,0:T(8,128)} %fusion.711, f32[576,3072]{1,0:T(8,128)} %fusion.712, f32[576,1536]{1,0:T(8,128)} %fusion.713), dimensions={1} | concatenate | bytes 28311552 | tf_op jit(solution)/shard_map/while/body/eval_jaxpr/concatenate | solution.py:249
  459.3 10.8 select_add_fusion.2
  478.7 16.8 %all-to-all-start = ((bf16[8,72,6144]{2,1,0:T(8,128)(2,1)}), bf16[8,72,6144]{2,1,0:T(8,128)(2,1)}, u32[]{:S(2)}, u32[]{:S(2)}) async-start(bf16[8,72,6144]{2,1,0:T(8,128)(2,1)} %stack.39), calls=%async_computation | async-start | bytes 14155776 | tf_op jit(solution)/shard_map/while/body/eval_jaxpr/all_to_all | solution.py:29
  497.1 176.4 %all-gather.4 = bf16[8,72,2]{1,2,0:T(2,128)(2,1)S(1)} all-gather(bf16[1,72,2]{1,2,0:T(2,128)(2,1)} %bitcast.589), channel_id=1, replica_groups=mesh['dp'=4,'fsdp'=8] {'fsdp'}, dimensions={0}, use_global_device_ids=true | all-gather | bytes 2592 | tf_op jit(solution)/shard_map/while/body/eval_jaxpr/all_gather | solution.py:299
  678.5 54.6 %all-to-all-done = bf16[8,72,6144]{2,1,0:T(8,128)(2,1)} async-done(((bf16[8,72,6144]{2,1,0:T(8,128)(2,1)}), bf16[8,72,6144]{2,1,0:T(8,128)(2,1)}, u32[]{:S(2)}, u32[]{:S(2)}) %all-to-all-start) | async-done | bytes 7077920 | tf_op jit(solution)/shard_map/while/body/eval_jaxpr/all_to_all | solution.py:29
  792.8 10.7 multiply_convert_fusion.11
  833.4 11.2 fusion.705
  860.3 13.2 fusion.702
  881.9 13.6 fusion.703
  910.3 15.8 %concatenate.101 = f32[576,6144]{1,0:T(8,128)} concatenate(f32[576,960]{1,0:T(8,128)} %fusion.710, f32[576,576]{1,0:T(8,128)} %fusion.711, f32[576,3072]{1,0:T(8,128)} %fusion.712, f32[576,1536]{1,0:T(8,128)} %fusion.713), dimensions={1} | concatenate | bytes 28311552 | tf_op jit(solution)/shard_map/while/body/eval_jaxpr/concatenate | solution.py:249
  926.0 15.2 select_add_fusion.2
  954.5 244.7 %reduce-scatter.3.cloned.1.call-done = f32[72,6144]{1,0:T(8,128)} async-done(((f32[576,6144]{1,0:T(8,128)}), f32[72,6144]{1,0:T(8,128)}) %reduce-scatter.3.cloned.1.call-update) | async-done | bytes 1769488 | tf_op jit(solution)/shard_map/reduce_scatter | solution.py:322
  1199.2 47.2 %all-reduce.5.cloned.1.call-done = f32[72,6144]{1,0:T(8,128)} async-done(((f32[72,6144]{1,0:T(8,128)}), f32[72,6144]{1,0:T(8,128)}) %all-reduce.5.cloned.1.call-update) | async-done | bytes 1769488 | tf_op jit(solution)/shard_map/psum | solution.py:325
  1250.9 64.5 %all-gather.9.cloned.1.call-done = f32[576,1536]{1,0:T(8,128)} async-done(((f32[72,1536]{1,0:T(8,128)}), f32[576,1536]{1,0:T(8,128)}) %all-gather.9.cloned.1.call-update) | async-done | bytes 3538960 | tf_op jit(solution)/shard_map/all_gather | solution.py:335
  1315.4 196.8 %conditional.1 = (f32[576,1536]{1,0:T(8,128)S(1)}) conditional(s32[]{:T(128)} %clamp.3, f32[576,1536]{1,0:T(8,128)} %all-gather.9.cloned.1.call-done, f32[576,1536]{1,0:T(8,128)} %all-gather.9.cloned.1.call-done, f32[576,1536]{1,0:T(8,128)} %all-gather.9.cloned.1.call-done, ...), branch_computations={%region_20.25_spmd, %region_25.27_spmd, %region_27.29_spmd, %regio... | conditional | flops 74772799488 | bytes 174001792 | solution.py:338
  1514.9 19.4 %all-reduce.2 = f32[576,2]{0,1:T(2,128)S(1)} all-reduce(f32[576,2]{0,1:T(2,128)S(1)} %copy-done.50), channel_id=3, replica_groups=mesh['dp'=4,'fsdp'=8] {'fsdp'}, use_global_device_ids=true, to_apply=%region_18.19.clone | all-reduce | flops 1152 | bytes 9216
  1540.7 16.3 %all-gather.1 = f32[8,72,2]{1,2,0:T(2,128)S(1)} all-gather(f32[1,72,2]{1,2,0:T(2,128)S(1)} %bitcast.638), channel_id=1, replica_groups=mesh['dp'=4,'fsdp'=8] {'fsdp'}, dimensions={0}, use_global_device_ids=true | all-gather | bytes 5184 | tf_op jit(solution)/shard_map/all_gather | solution.py:336
  (457 shorter events, 481.7 us)
Async XLA Ops:
  18.5 247.9 %all-to-all-start = ((bf16[8,72,6144]{2,1,0:T(8,128)(2,1)}), bf16[8,72,6144]{2,1,0:T(8,128)(2,1)}, u32[]{:S(2)}, u32[]{:S(2)}) async-start(bf16[8,72,6144]{2,1,0:T(8,128)(2,1)} %stack.39), calls=%async_computation | async-start | bytes 14155776 | tf_op jit(solution)/shard_map/while/body/eval_jaxpr/all_to_all | solution.py:29
  25.7 300.3 %all-gather.13.cloned.1.call-start = ((), (), s32[]{:S(2)}) async-start(), calls=%async_computation.6 | async-start | bytes 7962624 | tf_op jit(solution)/shard_map/while/body/eval_jaxpr/all_gather | solution.py:304
  209.0 60.8 %copy-start.46 = (f32[576]{0:T(1024)}, f32[576]{0:T(1024)S(1)}, u32[]{:S(2)}) copy-start(f32[576]{0:T(1024)S(1)} %get-tuple-element.458) | copy-start | bytes 6916 | tf_op jit(solution)/shard_map/while
  209.0 60.7 %copy-start.35 = (f32[1024]{0:T(1024)}, f32[1024]{0:T(1024)S(1)}, u32[]{:S(2)}) copy-start(f32[1024]{0:T(1024)S(1)} %add_rsqrt_fusion.4) | copy-start | bytes 12292 | tf_op jit(solution)/shard_map/while
  209.9 62.1 %copy-start.4 = (f32[1024,32]{0,1:T(8,128)}, f32[1024,32]{0,1:T(8,128)S(1)}, u32[]{:S(2)}) copy-start(f32[1024,32]{0,1:T(8,128)S(1)} %get-tuple-element.463) | copy-start | bytes 393220 | tf_op jit(solution)/shard_map/while
  209.9 62.1 %copy-start.6 = (f32[1024,32]{0,1:T(8,128)}, f32[1024,32]{0,1:T(8,128)S(1)}, u32[]{:S(2)}) copy-start(f32[1024,32]{0,1:T(8,128)S(1)} %get-tuple-element.462) | copy-start | bytes 393220 | tf_op jit(solution)/shard_map/while
  273.8 22.1 %copy-start.32 = (f32[3,3,512]{2,1,0:T(4,128)}, f32[3,3,512]{2,1,0:T(4,128)S(1)}, u32[]{:S(2)}) copy-start(f32[3,3,512]{2,1,0:T(4,128)S(1)} %get-tuple-element.474) | copy-start | bytes 55300 | tf_op jit(solution)/shard_map/while
  314.2 30.7 %copy-start.16 = (f32[1024,576]{0,1:T(8,128)}, f32[1024,576]{0,1:T(8,128)S(1)}, u32[]{:S(2)}) copy-start(f32[1024,576]{0,1:T(8,128)S(1)} %get-tuple-element.475) | copy-start | bytes 7077892 | tf_op jit(solution)/shard_map/while
  478.7 254.4 %all-to-all-start = ((bf16[8,72,6144]{2,1,0:T(8,128)(2,1)}), bf16[8,72,6144]{2,1,0:T(8,128)(2,1)}, u32[]{:S(2)}, u32[]{:S(2)}) async-start(bf16[8,72,6144]{2,1,0:T(8,128)(2,1)} %stack.39), calls=%async_computation | async-start | bytes 14155776 | tf_op jit(solution)/shard_map/while/body/eval_jaxpr/all_to_all | solution.py:29
  495.5 297.4 %all-gather.13.cloned.1.call-start = ((), (), s32[]{:S(2)}) async-start(), calls=%async_computation.6 | async-start | bytes 7962624 | tf_op jit(solution)/shard_map/while/body/eval_jaxpr/all_gather | solution.py:304
  677.2 59.4 %copy-start.46 = (f32[576]{0:T(1024)}, f32[576]{0:T(1024)S(1)}, u32[]{:S(2)}) copy-start(f32[576]{0:T(1024)S(1)} %get-tuple-element.458) | copy-start | bytes 6916 | tf_op jit(solution)/shard_map/while
  677.2 59.4 %copy-start.35 = (f32[1024]{0:T(1024)}, f32[1024]{0:T(1024)S(1)}, u32[]{:S(2)}) copy-start(f32[1024]{0:T(1024)S(1)} %add_rsqrt_fusion.4) | copy-start | bytes 12292 | tf_op jit(solution)/shard_map/while
  678.0 60.8 %copy-start.4 = (f32[1024,32]{0,1:T(8,128)}, f32[1024,32]{0,1:T(8,128)S(1)}, u32[]{:S(2)}) copy-start(f32[1024,32]{0,1:T(8,128)S(1)} %get-tuple-element.463) | copy-start | bytes 393220 | tf_op jit(solution)/shard_map/while
  678.0 60.8 %copy-start.6 = (f32[1024,32]{0,1:T(8,128)}, f32[1024,32]{0,1:T(8,128)S(1)}, u32[]{:S(2)}) copy-start(f32[1024,32]{0,1:T(8,128)S(1)} %get-tuple-element.462) | copy-start | bytes 393220 | tf_op jit(solution)/shard_map/while
  740.6 22.1 %copy-start.32 = (f32[3,3,512]{2,1,0:T(4,128)}, f32[3,3,512]{2,1,0:T(4,128)S(1)}, u32[]{:S(2)}) copy-start(f32[3,3,512]{2,1,0:T(4,128)S(1)} %get-tuple-element.474) | copy-start | bytes 55300 | tf_op jit(solution)/shard_map/while
  781.0 30.7 %copy-start.16 = (f32[1024,576]{0,1:T(8,128)}, f32[1024,576]{0,1:T(8,128)S(1)}, u32[]{:S(2)}) copy-start(f32[1024,576]{0,1:T(8,128)S(1)} %get-tuple-element.475) | copy-start | bytes 7077892 | tf_op jit(solution)/shard_map/while
  953.8 245.3 %reduce-scatter.3.cloned.1.call-start = ((), (), s32[]{:S(2)}) async-start(), calls=%async_computation.2 | async-start | bytes 15925248 | tf_op jit(solution)/shard_map/reduce_scatter | solution.py:322
  954.4 292.0 %copy-start.45 = (f32[72,6144]{1,0:T(8,128)S(1)}, f32[72,6144]{1,0:T(8,128)}, u32[]{:S(2)}) copy-start(f32[72,6144]{1,0:T(8,128)} %param.31) | copy-start | bytes 5308420
  954.4 292.0 %all-reduce.5.cloned.1.call-start = ((), (), s32[]{:S(2)}) async-start(), calls=%async_computation.3 | async-start | bytes 3538944 | tf_op jit(solution)/shard_map/psum | solution.py:325
  1199.2 116.2 %all-gather.9.cloned.1.call-start = ((), (), s32[]{:S(2)}) async-start(), calls=%async_computation.4 | async-start | bytes 3981312 | tf_op jit(solution)/shard_map/all_gather | solution.py:335
  1250.8 306.9 %all-gather.11.cloned.1.call-start = ((), (), s32[]{:S(2)}) async-start(), calls=%async_computation.5 | async-start | bytes 2211840 | tf_op jit(solution)/shard_map/all_gather | solution.py:344
  1315.4 199.5 %copy-start.50 = (f32[576,2]{0,1:T(2,128)S(1)}, f32[576,2]{0,1:T(2,128)}, u32[]{:S(2)}) copy-start(f32[576,2]{0,1:T(2,128)} %get-tuple-element.254) | copy-start | bytes 13828
  1315.4 224.7 %copy-start.53 = (f32[2,72]{1,0:T(2,128)S(1)}, f32[2,72]{1,0:T(2,128)}, u32[]{:S(2)}) copy-start(f32[2,72]{1,0:T(2,128)} %param.30) | copy-start | bytes 1732
  1315.4 241.7 %copy-start.52 = (f32[2,72]{1,0:T(2,128)S(1)}, f32[2,72]{1,0:T(2,128)}, u32[]{:S(2)}) copy-start(f32[2,72]{1,0:T(2,128)} %param.28) | copy-start | bytes 1732
  (96 other events, 552.9 us)
Sparse Core Ops, SparseCore 0:
  29.3 228.8 all-gather.12
  499.0 225.8 all-gather.12
Sparse Core Ops, SparseCore 1:
  957.9 241.1 reduce-scatter.2
  1201.4 44.9 all-reduce.4
  1250.9 64.4 all-gather.8
  1513.1 18.4 all-gather.10
